TPU v7x, 512 devices: a whole 4x4x16 slice. The times are simulated.
512 devices in a mesh: dom: 128 (over x, z, core), blk: 4 (over y).
Axes of the slice: x: 4, y: 4, z: 16, core: 2. Of those that a mesh axis runs over, the one named last changes fastest.
Arguments:
- degree: int32 [1024], P('dom'), may hold values from 1 to 3
- face_elem: int32 [4096], P('dom'), may hold values from 0 to 7
- face_side: int32 [4096], P('dom'), may hold values from 0 to 8, as said below
- face_peer: int32 [4096], P('dom'), may hold values from 0 to 7
- coupling: bfloat16 [4096, 320, 320], P('dom', 'blk'), may hold values from -0.078125 to 0.078125
- inv_diag: float32 [1024, 320], P('dom', 'blk'), may hold values from 0.5 to 2
- inv_off: bfloat16 [1024, 320, 320], P('dom', 'blk'), may hold values from -0.109375 to 0.109375
- source: float32 [1024, 320], P('dom', 'blk'), may hold values from -6 to 6
- residual: float32 [1024, 320], P('dom', 'blk'), may hold values from -0.6 to 0.6
Outputs:
- adjoint: float32 [1024, 320], P('dom', 'blk')
- indicator: float32 [1024], P('dom')
Inputs may be any that keep to these rules, and one draw needn't show every extreme that they name: `face_side`: among the 32 faces of one partition (aligned blocks of 32 rows) each side from 1 to 8 is named by at least 2 and at most 4 faces, and one side by exactly 4; the remaining faces have side 0.
All inputs are finite; a program needn't handle non-finite values.
Results may differ from a plain program's by a relative error of at most 0.004.
Values may be sent and summed in bfloat16 or wider, within the bound.
No kernel may reach another device: no remote copies, remote signals or barrier semaphores. Data moves between devices by JAX's collectives and lax.ppermute only.
A program may use at most 64 MiB of HBM per device.

v0:
```python
import jax
import jax.numpy as jnp
from jax import lax
from jax.sharding import PartitionSpec as P

MODES = 64
SWEEPS = 2
NEIGH = 8


def from_behind(block, axis, distance):
    devices = range(lax.axis_size(axis))
    route = [((i - distance) % len(devices), i) for i in devices]
    return lax.ppermute(block, axis, route)


def full_rows(values):
    return lax.all_gather(values, "blk", axis=1, tiled=True)


def local(degree, face_elem, face_side, face_peer, coupling, inv_diag, inv_off, source, residual):
    width = coupling.shape[2]
    quarter = source.shape[1]
    elements = source.shape[0]
    faces = coupling.shape[0]
    neigh = NEIGH
    half_count = neigh // 2
    capacity = faces // neigh
    offsets = [step_size for step_size in range(1, half_count + 1)] + [
        -step_size for step_size in range(1, half_count + 1)
    ]
    first_row = lax.axis_index("blk") * quarter
    limit = (degree + 1) ** 3 * MODES // 64
    modes = jnp.arange(width, dtype=jnp.int32) % MODES
    mask_full = (modes[None, :] < limit[:, None]).astype(jnp.float32)
    mask_rows = lax.dynamic_slice_in_dim(mask_full, first_row, quarter, 1)
    codes = jnp.arange(neigh + 1, dtype=jnp.int32)
    onehot = (face_side[:, None] == codes[None, :]).astype(jnp.int32)
    before = jnp.cumsum(onehot, axis=0) - onehot
    slot_index = jnp.sum(before * onehot, axis=1)
    crossing = face_side > 0
    inner = jnp.where(crossing, 0.0, 1.0).astype(jnp.float32)
    position = jnp.where(crossing, (face_side - 1) * capacity + slot_index, neigh * capacity)
    safe_position = jnp.minimum(position, neigh * capacity - 1)
    wanted = (
        jnp.zeros((neigh * capacity,), jnp.int32)
        .at[position]
        .set(face_peer, mode="drop")
        .reshape(neigh, capacity)
    )
    requested = jnp.stack(
        [from_behind(wanted[side_num], "dom", offsets[side_num]) for side_num in range(neigh)]
    )
    requested_flat = requested.reshape(-1)

    def invert(values_full):
        own_part = lax.dynamic_slice_in_dim(values_full, first_row, quarter, 1)
        product = jnp.einsum("eij,ej->ei", inv_off, values_full, preferred_element_type=jnp.float32)
        return inv_diag * own_part.astype(jnp.float32) + product

    source_half = (source * mask_rows).astype(jnp.bfloat16)
    base_state = invert(full_rows(source_half)) * mask_rows
    adjoint = base_state
    for sweep_index in range(SWEEPS):
        state_rows = adjoint.astype(jnp.bfloat16)
        state_full = full_rows(state_rows)
        outgoing = state_full[requested]
        incoming = jnp.stack(
            [
                from_behind(outgoing[side_num], "dom", -offsets[side_num])
                for side_num in range(neigh)
            ]
        ).reshape(-1, width)
        peer_state = jnp.where(crossing[:, None], incoming[safe_position], state_full[face_peer])
        elem_state = state_rows[face_elem]
        local_terms = jnp.einsum(
            "fij,fj->fi", coupling, peer_state, preferred_element_type=jnp.float32
        )
        transposed = jnp.einsum(
            "fij,fi->fj", coupling, elem_state, preferred_element_type=jnp.float32
        )
        own_terms = jnp.zeros((elements, quarter), jnp.float32).at[face_elem].add(local_terms)
        partial_value = (
            jnp.zeros((elements, width), jnp.float32).at[face_peer].add(transposed * inner[:, None])
        )
        outbound = (
            jnp.zeros((neigh * capacity, width), jnp.float32)
            .at[position]
            .set(transposed, mode="drop")
            .reshape(neigh, capacity, width)
        )
        returned = jnp.stack(
            [from_behind(outbound[side_num], "dom", offsets[side_num]) for side_num in range(neigh)]
        ).reshape(-1, width)
        partial_value = partial_value.at[requested_flat].add(returned)
        middle = lax.dynamic_slice_in_dim(partial_value, first_row, quarter, 1) + own_terms
        partial_value = lax.dynamic_update_slice_in_dim(partial_value, middle, first_row, 1)
        summed = lax.psum(partial_value, "blk")
        coupled_half = (summed * mask_full).astype(jnp.bfloat16)
        adjoint = (base_state - invert(coupled_half)) * mask_rows
    weights = jnp.sum(adjoint * residual * mask_rows, axis=1)
    indicator = lax.psum(weights, "blk")
    return (adjoint, indicator)


def solution(mesh):
    in_specs = (
        P("dom"),
        P("dom"),
        P("dom"),
        P("dom"),
        P("dom", "blk", None),
        P("dom", "blk"),
        P("dom", "blk", None),
        P("dom", "blk"),
        P("dom", "blk"),
    )
    out_specs = (P("dom", "blk"), P("dom"))
    return jax.shard_map(local, mesh=mesh, in_specs=in_specs, out_specs=out_specs, check_vma=False)
```

profile of v0, /device:TPU:64, one launch (start us, length us, event | category | flops | bytes accessed | tf_op | source)
XLA Modules:
  0.0 313.2 jit_solution(9358824529545259234)
XLA Ops:
  5.9 3.8 %collective-permute-start.1 = (s32[4]{0:T(128)S(1)}, s32[4]{0:T(128)S(1)}, u32[]{:S(2)}, u32[]{:S(2)}) collective-permute-start(s32[4]{0:T(128)S(1)} %get-tuple-element.44), channel_id=1, source_target_pairs={{504,0},{508,4},{0,8},{4,12},{8,16},{12,20},{16,24},{20,28},{24,32... | collective-permute-start | bytes 56 | tf_op jit(solution)/shard_map/ppermute | solution.py:14
  9.7 6.4 %collective-permute-start.2 = (s32[4]{0:T(128)S(1)}, s32[4]{0:T(128)S(1)}, u32[]{:S(2)}, u32[]{:S(2)}) collective-permute-start(s32[4]{0:T(128)S(1)} %get-tuple-element.43), channel_id=1, source_target_pairs={{500,0},{504,4},{508,8},{0,12},{4,16},{8,20},{12,24},{16,28},{20,3... | collective-permute-start | bytes 56 | tf_op jit(solution)/shard_map/ppermute | solution.py:14
  16.1 5.2 %collective-permute-start.3 = (s32[4]{0:T(128)S(1)}, s32[4]{0:T(128)S(1)}, u32[]{:S(2)}, u32[]{:S(2)}) collective-permute-start(s32[4]{0:T(128)S(1)} %get-tuple-element.42), channel_id=1, source_target_pairs={{496,0},{500,4},{504,8},{508,12},{0,16},{4,20},{8,24},{12,28},{16,... | collective-permute-start | bytes 56 | tf_op jit(solution)/shard_map/ppermute | solution.py:14
  26.7 11.3 %all-gather = bf16[4,80,8]{1,2,0:T(8,128)(2,1)S(1)} all-gather(bf16[1,80,8]{1,2,0:T(8,128)(2,1)S(1)} %fusion.36), channel_id=1, replica_groups=mesh['dom'=128,'blk'=4] {'blk'}, dimensions={0}, use_global_device_ids=true | all-gather | bytes 6400 | tf_op jit(solution)/shard_map/all_gather | solution.py:18
  43.5 10.4 %all-gather.1 = bf16[4,80,8]{1,2,0:T(8,128)(2,1)S(1)} all-gather(bf16[1,80,8]{1,2,0:T(8,128)(2,1)S(1)} %bitcast.165), channel_id=1, replica_groups=mesh['dom'=128,'blk'=4] {'blk'}, dimensions={0}, use_global_device_ids=true | all-gather | bytes 6400 | tf_op jit(solution)/shard_map/all_gather | solution.py:18
  58.7 5.2 %collective-permute-start.7 = (s32[4]{0:T(128)S(1)}, s32[4]{0:T(128)S(1)}, u32[]{:S(2)}, u32[]{:S(2)}) collective-permute-start(s32[4]{0:T(128)S(1)} %get-tuple-element.38), channel_id=1, source_target_pairs={{16,0},{20,4},{24,8},{28,12},{32,16},{36,20},{40,24},{44,28},{48,3... | collective-permute-start | bytes 56 | tf_op jit(solution)/shard_map/ppermute | solution.py:14
  63.9 3.5 %collective-permute-start.8 = (f32[4,320]{1,0:T(4,128)S(1)}, f32[4,320]{1,0:T(4,128)S(1)}, u32[]{:S(2)}, u32[]{:S(2)}) collective-permute-start(f32[4,320]{1,0:T(4,128)S(1)} %get-tuple-element.21), channel_id=1, source_target_pairs={{508,0},{0,4},{4,8},{8,12},{12,16},{16,20},{20,24},{24,28},{28,32}... | collective-permute-start | bytes 15368 | tf_op jit(solution)/shard_map/ppermute | solution.py:14
  69.6 3.9 %collective-permute-start.10 = (f32[4,320]{1,0:T(4,128)S(1)}, f32[4,320]{1,0:T(4,128)S(1)}, u32[]{:S(2)}, u32[]{:S(2)}) collective-permute-start(f32[4,320]{1,0:T(4,128)S(1)} %get-tuple-element.19), channel_id=1, source_target_pairs={{500,0},{504,4},{508,8},{0,12},{4,16},{8,20},{12,24},{16,28},{20,3... | collective-permute-start | bytes 15368 | tf_op jit(solution)/shard_map/ppermute | solution.py:14
  73.6 4.8 %collective-permute-start.11 = (f32[4,320]{1,0:T(4,128)S(1)}, f32[4,320]{1,0:T(4,128)S(1)}, u32[]{:S(2)}, u32[]{:S(2)}) collective-permute-start(f32[4,320]{1,0:T(4,128)S(1)} %get-tuple-element.18), channel_id=1, source_target_pairs={{496,0},{500,4},{504,8},{508,12},{0,16},{4,20},{8,24},{12,28},{16,... | collective-permute-start | bytes 15368 | tf_op jit(solution)/shard_map/ppermute | solution.py:14
  88.4 8.1 %collective-permute-start.18 = (bf16[4,320]{1,0:T(4,128)(2,1)S(1)}, bf16[4,320]{1,0:T(4,128)(2,1)S(1)}, u32[]{:S(2)}, u32[]{:S(2)}) collective-permute-start(bf16[4,320]{1,0:T(4,128)(2,1)S(1)} %get-tuple-element.35), channel_id=1, source_target_pairs={{12,0},{16,4},{20,8},{24,12},{28,16},{32,20},{36,24},{40,28},{44,3... | collective-permute-start | bytes 7688 | tf_op jit(solution)/shard_map/ppermute | solution.py:14
  97.8 3.6 %collective-permute-start.19 = (bf16[4,320]{1,0:T(4,128)(2,1)S(1)}, bf16[4,320]{1,0:T(4,128)(2,1)S(1)}, u32[]{:S(2)}, u32[]{:S(2)}) collective-permute-start(bf16[4,320]{1,0:T(4,128)(2,1)S(1)} %get-tuple-element.34), channel_id=1, source_target_pairs={{16,0},{20,4},{24,8},{28,12},{32,16},{36,20},{40,24},{44,28},{48,3... | collective-permute-start | bytes 7688 | tf_op jit(solution)/shard_map/ppermute | solution.py:14
  101.5 4.0 %collective-permute-done.19 = bf16[4,320]{1,0:T(4,128)(2,1)S(1)} collective-permute-done((bf16[4,320]{1,0:T(4,128)(2,1)S(1)}, bf16[4,320]{1,0:T(4,128)(2,1)S(1)}, u32[]{:S(2)}, u32[]{:S(2)}) %collective-permute-start.19) | collective-permute-done | bytes 2592 | tf_op jit(solution)/shard_map/ppermute | solution.py:14
  107.4 7.2 %collective-permute-done.20 = bf16[4,320]{1,0:T(4,128)(2,1)S(1)} collective-permute-done((bf16[4,320]{1,0:T(4,128)(2,1)S(1)}, bf16[4,320]{1,0:T(4,128)(2,1)S(1)}, u32[]{:S(2)}, u32[]{:S(2)}) %collective-permute-start.20) | collective-permute-done | bytes 2592 | tf_op jit(solution)/shard_map/ppermute | solution.py:14
  116.5 3.5 %collective-permute-done.21 = bf16[4,320]{1,0:T(4,128)(2,1)S(1)} collective-permute-done((bf16[4,320]{1,0:T(4,128)(2,1)S(1)}, bf16[4,320]{1,0:T(4,128)(2,1)S(1)}, u32[]{:S(2)}, u32[]{:S(2)}) %collective-permute-start.21) | collective-permute-done | bytes 2592 | tf_op jit(solution)/shard_map/ppermute | solution.py:14
  122.0 4.4 %collective-permute-done.22 = bf16[4,320]{1,0:T(4,128)(2,1)S(1)} collective-permute-done((bf16[4,320]{1,0:T(4,128)(2,1)S(1)}, bf16[4,320]{1,0:T(4,128)(2,1)S(1)}, u32[]{:S(2)}, u32[]{:S(2)}) %collective-permute-start.22) | collective-permute-done | bytes 2592 | tf_op jit(solution)/shard_map/ppermute | solution.py:14
  128.6 13.6 %collective-permute-done.23 = bf16[4,320]{1,0:T(4,128)(2,1)S(1)} collective-permute-done((bf16[4,320]{1,0:T(4,128)(2,1)S(1)}, bf16[4,320]{1,0:T(4,128)(2,1)S(1)}, u32[]{:S(2)}, u32[]{:S(2)}) %collective-permute-start.23) | collective-permute-done | bytes 2592 | tf_op jit(solution)/shard_map/ppermute | solution.py:14
  145.6 3.4 %collective-permute-start.13 = (f32[4,320]{1,0:T(4,128)S(1)}, f32[4,320]{1,0:T(4,128)S(1)}, u32[]{:S(2)}, u32[]{:S(2)}) collective-permute-start(f32[4,320]{1,0:T(4,128)S(1)} %get-tuple-element.16), channel_id=1, source_target_pairs={{8,0},{12,4},{16,8},{20,12},{24,16},{28,20},{32,24},{36,28},{40,32... | collective-permute-start | bytes 15368 | tf_op jit(solution)/shard_map/ppermute | solution.py:14
  149.0 6.8 %collective-permute-start.14 = (f32[4,320]{1,0:T(4,128)S(1)}, f32[4,320]{1,0:T(4,128)S(1)}, u32[]{:S(2)}, u32[]{:S(2)}) collective-permute-start(f32[4,320]{1,0:T(4,128)S(1)} %get-tuple-element.15), channel_id=1, source_target_pairs={{12,0},{16,4},{20,8},{24,12},{28,16},{32,20},{36,24},{40,28},{44,3... | collective-permute-start | bytes 15368 | tf_op jit(solution)/shard_map/ppermute | solution.py:14
  157.9 5.6 %collective-permute-done.15 = f32[4,320]{1,0:T(4,128)S(1)} collective-permute-done((f32[4,320]{1,0:T(4,128)S(1)}, f32[4,320]{1,0:T(4,128)S(1)}, u32[]{:S(2)}, u32[]{:S(2)}) %collective-permute-start.15) | collective-permute-done | bytes 5152 | tf_op jit(solution)/shard_map/ppermute | solution.py:14
  165.4 15.8 %psum.21 = bf16[8,320]{1,0:T(8,128)(2,1)S(1)} all-reduce(f32[8,320]{1,0:T(8,128)S(1)} %dynamic_update_slice.6), channel_id=1, replica_groups=mesh['dom'=128,'blk'=4] {'blk'}, use_global_device_ids=true, to_apply=%region_7.8 | all-reduce | flops 2560 | bytes 15360 | tf_op jit(solution)/shard_map/psum | solution.py:98
  183.4 10.4 %all-gather.2 = bf16[4,80,8]{1,2,0:T(8,128)(2,1)S(1)} all-gather(bf16[1,80,8]{1,2,0:T(8,128)(2,1)S(1)} %bitcast.166), channel_id=1, replica_groups=mesh['dom'=128,'blk'=4] {'blk'}, dimensions={0}, use_global_device_ids=true | all-gather | bytes 6400 | tf_op jit(solution)/shard_map/all_gather | solution.py:18
  200.5 3.6 %collective-permute-start.25 = (f32[4,320]{1,0:T(4,128)S(1)}, f32[4,320]{1,0:T(4,128)S(1)}, u32[]{:S(2)}, u32[]{:S(2)}) collective-permute-start(f32[4,320]{1,0:T(4,128)S(1)} %get-tuple-element.12), channel_id=1, source_target_pairs={{504,0},{508,4},{0,8},{4,12},{8,16},{12,20},{16,24},{20,28},{24,32... | collective-permute-start | bytes 15368 | tf_op jit(solution)/shard_map/ppermute | solution.py:14
  213.5 5.9 %collective-permute-start.34 = (bf16[4,320]{1,0:T(4,128)(2,1)S(1)}, bf16[4,320]{1,0:T(4,128)(2,1)S(1)}, u32[]{:S(2)}, u32[]{:S(2)}) collective-permute-start(bf16[4,320]{1,0:T(4,128)(2,1)S(1)} %get-tuple-element.27), channel_id=1, source_target_pairs={{12,0},{16,4},{20,8},{24,12},{28,16},{32,20},{36,24},{40,28},{44,3... | collective-permute-start | bytes 7688 | tf_op jit(solution)/shard_map/ppermute | solution.py:14
  220.7 5.3 %collective-permute-start.35 = (bf16[4,320]{1,0:T(4,128)(2,1)S(1)}, bf16[4,320]{1,0:T(4,128)(2,1)S(1)}, u32[]{:S(2)}, u32[]{:S(2)}) collective-permute-start(bf16[4,320]{1,0:T(4,128)(2,1)S(1)} %get-tuple-element.26), channel_id=1, source_target_pairs={{16,0},{20,4},{24,8},{28,12},{32,16},{36,20},{40,24},{44,28},{48,3... | collective-permute-start | bytes 7688 | tf_op jit(solution)/shard_map/ppermute | solution.py:14
  231.4 6.0 %collective-permute-done.36 = bf16[4,320]{1,0:T(4,128)(2,1)S(1)} collective-permute-done((bf16[4,320]{1,0:T(4,128)(2,1)S(1)}, bf16[4,320]{1,0:T(4,128)(2,1)S(1)}, u32[]{:S(2)}, u32[]{:S(2)}) %collective-permute-start.36) | collective-permute-done | bytes 2592 | tf_op jit(solution)/shard_map/ppermute | solution.py:14
  239.3 4.8 %collective-permute-done.37 = bf16[4,320]{1,0:T(4,128)(2,1)S(1)} collective-permute-done((bf16[4,320]{1,0:T(4,128)(2,1)S(1)}, bf16[4,320]{1,0:T(4,128)(2,1)S(1)}, u32[]{:S(2)}, u32[]{:S(2)}) %collective-permute-start.37) | collective-permute-done | bytes 2592 | tf_op jit(solution)/shard_map/ppermute | solution.py:14
  246.1 4.6 %collective-permute-done.38 = bf16[4,320]{1,0:T(4,128)(2,1)S(1)} collective-permute-done((bf16[4,320]{1,0:T(4,128)(2,1)S(1)}, bf16[4,320]{1,0:T(4,128)(2,1)S(1)}, u32[]{:S(2)}, u32[]{:S(2)}) %collective-permute-start.38) | collective-permute-done | bytes 2592 | tf_op jit(solution)/shard_map/ppermute | solution.py:14
  252.7 12.3 %collective-permute-done.39 = bf16[4,320]{1,0:T(4,128)(2,1)S(1)} collective-permute-done((bf16[4,320]{1,0:T(4,128)(2,1)S(1)}, bf16[4,320]{1,0:T(4,128)(2,1)S(1)}, u32[]{:S(2)}, u32[]{:S(2)}) %collective-permute-start.39) | collective-permute-done | bytes 2592 | tf_op jit(solution)/shard_map/ppermute | solution.py:14
  271.9 6.8 %collective-permute-start.30 = (f32[4,320]{1,0:T(4,128)S(1)}, f32[4,320]{1,0:T(4,128)S(1)}, u32[]{:S(2)}, u32[]{:S(2)}) collective-permute-start(f32[4,320]{1,0:T(4,128)S(1)} %get-tuple-element.7), channel_id=1, source_target_pairs={{12,0},{16,4},{20,8},{24,12},{28,16},{32,20},{36,24},{40,28},{44,3... | collective-permute-start | bytes 15368 | tf_op jit(solution)/shard_map/ppermute | solution.py:14
  280.7 5.6 %collective-permute-done.31 = f32[4,320]{1,0:T(4,128)S(1)} collective-permute-done((f32[4,320]{1,0:T(4,128)S(1)}, f32[4,320]{1,0:T(4,128)S(1)}, u32[]{:S(2)}, u32[]{:S(2)}) %collective-permute-start.31) | collective-permute-done | bytes 5152 | tf_op jit(solution)/shard_map/ppermute | solution.py:14
  288.2 14.3 %psum.22 = bf16[8,320]{1,0:T(8,128)(2,1)S(1)} all-reduce(f32[8,320]{1,0:T(8,128)S(1)} %dynamic_update_slice.7), channel_id=1, replica_groups=mesh['dom'=128,'blk'=4] {'blk'}, use_global_device_ids=true, to_apply=%region_12.13 | all-reduce | flops 2560 | bytes 15360 | tf_op jit(solution)/shard_map/psum | solution.py:98
  303.7 9.5 %psum.23 = f32[8]{0:T(128)} all-reduce(f32[8]{0:T(128)S(1)} %get-tuple-element.2), channel_id=1, replica_groups=mesh['dom'=128,'blk'=4] {'blk'}, use_global_device_ids=true, to_apply=%region_14.15 | all-reduce | flops 8 | bytes 64 | tf_op jit(solution)/shard_map/psum | solution.py:102
  (176 shorter events, 91.8 us)
Async XLA Ops:
  4.0 50.7 %collective-permute-start = (s32[4]{0:T(128)S(1)}, s32[4]{0:T(128)S(1)}, u32[]{:S(2)}, u32[]{:S(2)}) collective-permute-start(s32[4]{0:T(128)S(1)} %get-tuple-element.45), channel_id=1, source_target_pairs={{508,0},{0,4},{4,8},{8,12},{12,16},{16,20},{20,24},{24,28},{28,32}... | collective-permute-start | bytes 56 | tf_op jit(solution)/shard_map/ppermute | solution.py:14
  5.9 50.8 %collective-permute-start.1 = (s32[4]{0:T(128)S(1)}, s32[4]{0:T(128)S(1)}, u32[]{:S(2)}, u32[]{:S(2)}) collective-permute-start(s32[4]{0:T(128)S(1)} %get-tuple-element.44), channel_id=1, source_target_pairs={{504,0},{508,4},{0,8},{4,12},{8,16},{12,20},{16,24},{20,28},{24,32... | collective-permute-start | bytes 56 | tf_op jit(solution)/shard_map/ppermute | solution.py:14
  9.7 48.9 %collective-permute-start.2 = (s32[4]{0:T(128)S(1)}, s32[4]{0:T(128)S(1)}, u32[]{:S(2)}, u32[]{:S(2)}) collective-permute-start(s32[4]{0:T(128)S(1)} %get-tuple-element.43), channel_id=1, source_target_pairs={{500,0},{504,4},{508,8},{0,12},{4,16},{8,20},{12,24},{16,28},{20,3... | collective-permute-start | bytes 56 | tf_op jit(solution)/shard_map/ppermute | solution.py:14
  16.1 47.8 %collective-permute-start.3 = (s32[4]{0:T(128)S(1)}, s32[4]{0:T(128)S(1)}, u32[]{:S(2)}, u32[]{:S(2)}) collective-permute-start(s32[4]{0:T(128)S(1)} %get-tuple-element.42), channel_id=1, source_target_pairs={{496,0},{500,4},{504,8},{508,12},{0,16},{4,20},{8,24},{12,28},{16,... | collective-permute-start | bytes 56 | tf_op jit(solution)/shard_map/ppermute | solution.py:14
  21.3 46.1 %collective-permute-start.4 = (s32[4]{0:T(128)S(1)}, s32[4]{0:T(128)S(1)}, u32[]{:S(2)}, u32[]{:S(2)}) collective-permute-start(s32[4]{0:T(128)S(1)} %get-tuple-element.41), channel_id=1, source_target_pairs={{4,0},{8,4},{12,8},{16,12},{20,16},{24,20},{28,24},{32,28},{36,32}... | collective-permute-start | bytes 56 | tf_op jit(solution)/shard_map/ppermute | solution.py:14
  54.7 14.9 %collective-permute-start.5 = (s32[4]{0:T(128)S(1)}, s32[4]{0:T(128)S(1)}, u32[]{:S(2)}, u32[]{:S(2)}) collective-permute-start(s32[4]{0:T(128)S(1)} %get-tuple-element.40), channel_id=1, source_target_pairs={{8,0},{12,4},{16,8},{20,12},{24,16},{28,20},{32,24},{36,28},{40,32... | collective-permute-start | bytes 56 | tf_op jit(solution)/shard_map/ppermute | solution.py:14
  56.7 16.8 %collective-permute-start.6 = (s32[4]{0:T(128)S(1)}, s32[4]{0:T(128)S(1)}, u32[]{:S(2)}, u32[]{:S(2)}) collective-permute-start(s32[4]{0:T(128)S(1)} %get-tuple-element.39), channel_id=1, source_target_pairs={{12,0},{16,4},{20,8},{24,12},{28,16},{32,20},{36,24},{40,28},{44,3... | collective-permute-start | bytes 56 | tf_op jit(solution)/shard_map/ppermute | solution.py:14
  58.7 19.7 %collective-permute-start.7 = (s32[4]{0:T(128)S(1)}, s32[4]{0:T(128)S(1)}, u32[]{:S(2)}, u32[]{:S(2)}) collective-permute-start(s32[4]{0:T(128)S(1)} %get-tuple-element.38), channel_id=1, source_target_pairs={{16,0},{20,4},{24,8},{28,12},{32,16},{36,20},{40,24},{44,28},{48,3... | collective-permute-start | bytes 56 | tf_op jit(solution)/shard_map/ppermute | solution.py:14
  63.9 81.7 %collective-permute-start.8 = (f32[4,320]{1,0:T(4,128)S(1)}, f32[4,320]{1,0:T(4,128)S(1)}, u32[]{:S(2)}, u32[]{:S(2)}) collective-permute-start(f32[4,320]{1,0:T(4,128)S(1)} %get-tuple-element.21), channel_id=1, source_target_pairs={{508,0},{0,4},{4,8},{8,12},{12,16},{16,20},{20,24},{24,28},{28,32}... | collective-permute-start | bytes 15368 | tf_op jit(solution)/shard_map/ppermute | solution.py:14
  67.4 81.6 %collective-permute-start.9 = (f32[4,320]{1,0:T(4,128)S(1)}, f32[4,320]{1,0:T(4,128)S(1)}, u32[]{:S(2)}, u32[]{:S(2)}) collective-permute-start(f32[4,320]{1,0:T(4,128)S(1)} %get-tuple-element.20), channel_id=1, source_target_pairs={{504,0},{508,4},{0,8},{4,12},{8,16},{12,20},{16,24},{20,28},{24,32... | collective-permute-start | bytes 15368 | tf_op jit(solution)/shard_map/ppermute | solution.py:14
  69.6 86.2 %collective-permute-start.10 = (f32[4,320]{1,0:T(4,128)S(1)}, f32[4,320]{1,0:T(4,128)S(1)}, u32[]{:S(2)}, u32[]{:S(2)}) collective-permute-start(f32[4,320]{1,0:T(4,128)S(1)} %get-tuple-element.19), channel_id=1, source_target_pairs={{500,0},{504,4},{508,8},{0,12},{4,16},{8,20},{12,24},{16,28},{20,3... | collective-permute-start | bytes 15368 | tf_op jit(solution)/shard_map/ppermute | solution.py:14
  73.6 84.2 %collective-permute-start.11 = (f32[4,320]{1,0:T(4,128)S(1)}, f32[4,320]{1,0:T(4,128)S(1)}, u32[]{:S(2)}, u32[]{:S(2)}) collective-permute-start(f32[4,320]{1,0:T(4,128)S(1)} %get-tuple-element.18), channel_id=1, source_target_pairs={{496,0},{500,4},{504,8},{508,12},{0,16},{4,20},{8,24},{12,28},{16,... | collective-permute-start | bytes 15368 | tf_op jit(solution)/shard_map/ppermute | solution.py:14
  88.4 9.4 %collective-permute-start.18 = (bf16[4,320]{1,0:T(4,128)(2,1)S(1)}, bf16[4,320]{1,0:T(4,128)(2,1)S(1)}, u32[]{:S(2)}, u32[]{:S(2)}) collective-permute-start(bf16[4,320]{1,0:T(4,128)(2,1)S(1)} %get-tuple-element.35), channel_id=1, source_target_pairs={{12,0},{16,4},{20,8},{24,12},{28,16},{32,20},{36,24},{40,28},{44,3... | collective-permute-start | bytes 7688 | tf_op jit(solution)/shard_map/ppermute | solution.py:14
  97.8 7.6 %collective-permute-start.19 = (bf16[4,320]{1,0:T(4,128)(2,1)S(1)}, bf16[4,320]{1,0:T(4,128)(2,1)S(1)}, u32[]{:S(2)}, u32[]{:S(2)}) collective-permute-start(bf16[4,320]{1,0:T(4,128)(2,1)S(1)} %get-tuple-element.34), channel_id=1, source_target_pairs={{16,0},{20,4},{24,8},{28,12},{32,16},{36,20},{40,24},{44,28},{48,3... | collective-permute-start | bytes 7688 | tf_op jit(solution)/shard_map/ppermute | solution.py:14
  105.4 9.2 %collective-permute-start.20 = (bf16[4,320]{1,0:T(4,128)(2,1)S(1)}, bf16[4,320]{1,0:T(4,128)(2,1)S(1)}, u32[]{:S(2)}, u32[]{:S(2)}) collective-permute-start(bf16[4,320]{1,0:T(4,128)(2,1)S(1)} %get-tuple-element.33), channel_id=1, source_target_pairs={{508,0},{0,4},{4,8},{8,12},{12,16},{16,20},{20,24},{24,28},{28,32}... | collective-permute-start | bytes 7688 | tf_op jit(solution)/shard_map/ppermute | solution.py:14
  126.4 15.7 %collective-permute-start.23 = (bf16[4,320]{1,0:T(4,128)(2,1)S(1)}, bf16[4,320]{1,0:T(4,128)(2,1)S(1)}, u32[]{:S(2)}, u32[]{:S(2)}) collective-permute-start(bf16[4,320]{1,0:T(4,128)(2,1)S(1)} %get-tuple-element.30), channel_id=1, source_target_pairs={{496,0},{500,4},{504,8},{508,12},{0,16},{4,20},{8,24},{12,28},{16,... | collective-permute-start | bytes 7688 | tf_op jit(solution)/shard_map/ppermute | solution.py:14
  142.2 15.6 %collective-permute-start.12 = (f32[4,320]{1,0:T(4,128)S(1)}, f32[4,320]{1,0:T(4,128)S(1)}, u32[]{:S(2)}, u32[]{:S(2)}) collective-permute-start(f32[4,320]{1,0:T(4,128)S(1)} %get-tuple-element.17), channel_id=1, source_target_pairs={{4,0},{8,4},{12,8},{16,12},{20,16},{24,20},{28,24},{32,28},{36,32}... | collective-permute-start | bytes 15368 | tf_op jit(solution)/shard_map/ppermute | solution.py:14
  145.6 12.2 %collective-permute-start.13 = (f32[4,320]{1,0:T(4,128)S(1)}, f32[4,320]{1,0:T(4,128)S(1)}, u32[]{:S(2)}, u32[]{:S(2)}) collective-permute-start(f32[4,320]{1,0:T(4,128)S(1)} %get-tuple-element.16), channel_id=1, source_target_pairs={{8,0},{12,4},{16,8},{20,12},{24,16},{28,20},{32,24},{36,28},{40,32... | collective-permute-start | bytes 15368 | tf_op jit(solution)/shard_map/ppermute | solution.py:14
  149.0 8.8 %collective-permute-start.14 = (f32[4,320]{1,0:T(4,128)S(1)}, f32[4,320]{1,0:T(4,128)S(1)}, u32[]{:S(2)}, u32[]{:S(2)}) collective-permute-start(f32[4,320]{1,0:T(4,128)S(1)} %get-tuple-element.15), channel_id=1, source_target_pairs={{12,0},{16,4},{20,8},{24,12},{28,16},{32,20},{36,24},{40,28},{44,3... | collective-permute-start | bytes 15368 | tf_op jit(solution)/shard_map/ppermute | solution.py:14
  155.9 7.6 %collective-permute-start.15 = (f32[4,320]{1,0:T(4,128)S(1)}, f32[4,320]{1,0:T(4,128)S(1)}, u32[]{:S(2)}, u32[]{:S(2)}) collective-permute-start(f32[4,320]{1,0:T(4,128)S(1)} %get-tuple-element.14), channel_id=1, source_target_pairs={{16,0},{20,4},{24,8},{28,12},{32,16},{36,20},{40,24},{44,28},{48,3... | collective-permute-start | bytes 15368 | tf_op jit(solution)/shard_map/ppermute | solution.py:14
  194.6 13.3 %collective-permute-start.32 = (bf16[4,320]{1,0:T(4,128)(2,1)S(1)}, bf16[4,320]{1,0:T(4,128)(2,1)S(1)}, u32[]{:S(2)}, u32[]{:S(2)}) collective-permute-start(bf16[4,320]{1,0:T(4,128)(2,1)S(1)} %get-tuple-element.29), channel_id=1, source_target_pairs={{4,0},{8,4},{12,8},{16,12},{20,16},{24,20},{28,24},{32,28},{36,32}... | collective-permute-start | bytes 7688 | tf_op jit(solution)/shard_map/ppermute | solution.py:14
  198.0 70.4 %collective-permute-start.24 = (f32[4,320]{1,0:T(4,128)S(1)}, f32[4,320]{1,0:T(4,128)S(1)}, u32[]{:S(2)}, u32[]{:S(2)}) collective-permute-start(f32[4,320]{1,0:T(4,128)S(1)} %get-tuple-element.13), channel_id=1, source_target_pairs={{508,0},{0,4},{4,8},{8,12},{12,16},{16,20},{20,24},{24,28},{28,32}... | collective-permute-start | bytes 15368 | tf_op jit(solution)/shard_map/ppermute | solution.py:14
  200.5 71.4 %collective-permute-start.25 = (f32[4,320]{1,0:T(4,128)S(1)}, f32[4,320]{1,0:T(4,128)S(1)}, u32[]{:S(2)}, u32[]{:S(2)}) collective-permute-start(f32[4,320]{1,0:T(4,128)S(1)} %get-tuple-element.12), channel_id=1, source_target_pairs={{504,0},{508,4},{0,8},{4,12},{8,16},{12,20},{16,24},{20,28},{24,32... | collective-permute-start | bytes 15368 | tf_op jit(solution)/shard_map/ppermute | solution.py:14
  204.1 74.6 %collective-permute-start.26 = (f32[4,320]{1,0:T(4,128)S(1)}, f32[4,320]{1,0:T(4,128)S(1)}, u32[]{:S(2)}, u32[]{:S(2)}) collective-permute-start(f32[4,320]{1,0:T(4,128)S(1)} %get-tuple-element.11), channel_id=1, source_target_pairs={{500,0},{504,4},{508,8},{0,12},{4,16},{8,20},{12,24},{16,28},{20,3... | collective-permute-start | bytes 15368 | tf_op jit(solution)/shard_map/ppermute | solution.py:14
  206.0 74.6 %collective-permute-start.27 = (f32[4,320]{1,0:T(4,128)S(1)}, f32[4,320]{1,0:T(4,128)S(1)}, u32[]{:S(2)}, u32[]{:S(2)}) collective-permute-start(f32[4,320]{1,0:T(4,128)S(1)} %get-tuple-element.10), channel_id=1, source_target_pairs={{496,0},{500,4},{504,8},{508,12},{0,16},{4,20},{8,24},{12,28},{16,... | collective-permute-start | bytes 15368 | tf_op jit(solution)/shard_map/ppermute | solution.py:14
  220.7 7.6 %collective-permute-start.35 = (bf16[4,320]{1,0:T(4,128)(2,1)S(1)}, bf16[4,320]{1,0:T(4,128)(2,1)S(1)}, u32[]{:S(2)}, u32[]{:S(2)}) collective-permute-start(bf16[4,320]{1,0:T(4,128)(2,1)S(1)} %get-tuple-element.26), channel_id=1, source_target_pairs={{16,0},{20,4},{24,8},{28,12},{32,16},{36,20},{40,24},{44,28},{48,3... | collective-permute-start | bytes 7688 | tf_op jit(solution)/shard_map/ppermute | solution.py:14
  228.3 9.2 %collective-permute-start.36 = (bf16[4,320]{1,0:T(4,128)(2,1)S(1)}, bf16[4,320]{1,0:T(4,128)(2,1)S(1)}, u32[]{:S(2)}, u32[]{:S(2)}) collective-permute-start(bf16[4,320]{1,0:T(4,128)(2,1)S(1)} %get-tuple-element.25), channel_id=1, source_target_pairs={{508,0},{0,4},{4,8},{8,12},{12,16},{16,20},{20,24},{24,28},{28,32}... | collective-permute-start | bytes 7688 | tf_op jit(solution)/shard_map/ppermute | solution.py:14
  250.7 14.3 %collective-permute-start.39 = (bf16[4,320]{1,0:T(4,128)(2,1)S(1)}, bf16[4,320]{1,0:T(4,128)(2,1)S(1)}, u32[]{:S(2)}, u32[]{:S(2)}) collective-permute-start(bf16[4,320]{1,0:T(4,128)(2,1)S(1)} %get-tuple-element.22), channel_id=1, source_target_pairs={{496,0},{500,4},{504,8},{508,12},{0,16},{4,20},{8,24},{12,28},{16,... | collective-permute-start | bytes 7688 | tf_op jit(solution)/shard_map/ppermute | solution.py:14
  265.0 15.6 %collective-permute-start.28 = (f32[4,320]{1,0:T(4,128)S(1)}, f32[4,320]{1,0:T(4,128)S(1)}, u32[]{:S(2)}, u32[]{:S(2)}) collective-permute-start(f32[4,320]{1,0:T(4,128)S(1)} %get-tuple-element.9), channel_id=1, source_target_pairs={{4,0},{8,4},{12,8},{16,12},{20,16},{24,20},{28,24},{32,28},{36,32}... | collective-permute-start | bytes 15368 | tf_op jit(solution)/shard_map/ppermute | solution.py:14
  268.4 12.2 %collective-permute-start.29 = (f32[4,320]{1,0:T(4,128)S(1)}, f32[4,320]{1,0:T(4,128)S(1)}, u32[]{:S(2)}, u32[]{:S(2)}) collective-permute-start(f32[4,320]{1,0:T(4,128)S(1)} %get-tuple-element.8), channel_id=1, source_target_pairs={{8,0},{12,4},{16,8},{20,12},{24,16},{28,20},{32,24},{36,28},{40,32... | collective-permute-start | bytes 15368 | tf_op jit(solution)/shard_map/ppermute | solution.py:14
  271.9 8.8 %collective-permute-start.30 = (f32[4,320]{1,0:T(4,128)S(1)}, f32[4,320]{1,0:T(4,128)S(1)}, u32[]{:S(2)}, u32[]{:S(2)}) collective-permute-start(f32[4,320]{1,0:T(4,128)S(1)} %get-tuple-element.7), channel_id=1, source_target_pairs={{12,0},{16,4},{20,8},{24,12},{28,16},{32,20},{36,24},{40,28},{44,3... | collective-permute-start | bytes 15368 | tf_op jit(solution)/shard_map/ppermute | solution.py:14
  278.7 7.6 %collective-permute-start.31 = (f32[4,320]{1,0:T(4,128)S(1)}, f32[4,320]{1,0:T(4,128)S(1)}, u32[]{:S(2)}, u32[]{:S(2)}) collective-permute-start(f32[4,320]{1,0:T(4,128)S(1)} %get-tuple-element.6), channel_id=1, source_target_pairs={{16,0},{20,4},{24,8},{28,12},{32,16},{36,20},{40,24},{44,28},{48,3... | collective-permute-start | bytes 15368 | tf_op jit(solution)/shard_map/ppermute | solution.py:14
  (12 other events, 261.7 us)
where the time goes:
time: 315 us; the launch traced here: 313 us
  starting transfers between devices  130 us (41%)
  waiting for transfers between devices  83.1 us (26%)
  blocking collectives  71.8 us (23%)
  other arithmetic  13.5 us (4%)
  local copies, waits for them, and re-layouts  8.94 us (3%)
  matrix products  4.21 us (1%)
    ppermute x40, starting transfers between devices, from_behind(): return lax.ppermute(block, axis, route)  130 us
    ppermute x40, waiting for transfers between devices, from_behind(): return lax.ppermute(block, axis, route)  83.1 us
    all_gather x3, blocking collectives, full_rows(): return lax.all_gather(values, 'blk', axis=1, tiled=True)  32.2 us
    psum x2, blocking collectives, local(): summed = lax.psum(partial_value, 'blk')  30.1 us
    psum x1, blocking collectives, local(): indicator = lax.psum(weights, 'blk')  9.47 us
  transfers between devices with their start and end apart: 40, of which 17 were waited for; matrix products, arithmetic and copies ran while one was open for 5% of the time, Pallas kernels for 0%

commit v1 on v0

--- a/solution.py
+++ b/solution.py
@@ -15,7 +15,8 @@
 
 
 def full_rows(values):
-    return lax.all_gather(values, "blk", axis=1, tiled=True)
+    show_surface = lambda state: jnp.concatenate(lax.all_gather(state, "blk"), 1)
+    return show_surface(values)
 
 
 def local(degree, face_elem, face_side, face_peer, coupling, inv_diag, inv_off, source, residual):

time: 315 us -> 314 us (level)
  no operation moved by 1% of the time
where the time goes in v1:
time: 314 us; the launch traced here: 313 us
  starting transfers between devices  130 us (41%)
  waiting for transfers between devices  83.1 us (26%)
  blocking collectives  71.7 us (23%)
  other arithmetic  12.8 us (4%)
  local copies, waits for them, and re-layouts  9.03 us (3%)
  matrix products  4.21 us (1%)
    ppermute x40, starting transfers between devices, from_behind(): return lax.ppermute(block, axis, route)  130 us
    ppermute x40, waiting for transfers between devices, from_behind(): return lax.ppermute(block, axis, route)  83.1 us
    all_gather x3, blocking collectives, full_rows(): lax.all_gather(state, 'blk')  32.2 us
    psum x2, blocking collectives, local(): summed = lax.psum(partial_value, 'blk')  30.1 us
    psum x1, blocking collectives, local(): indicator = lax.psum(weights, 'blk')  9.47 us
  transfers between devices with their start and end apart: 40, of which 17 were waited for; matrix products, arithmetic and copies ran while one was open for 5% of the time, Pallas kernels for 0%

profile of v1, /device:TPU:64, one launch (start us, length us, event | category | flops | bytes accessed | tf_op | source)
XLA Modules:
  0.0 312.6 jit_solution(11335333235190075278)
XLA Ops:
  5.9 3.8 %collective-permute-start.1 = (s32[4]{0:T(128)S(1)}, s32[4]{0:T(128)S(1)}, u32[]{:S(2)}, u32[]{:S(2)}) collective-permute-start(s32[4]{0:T(128)S(1)} %get-tuple-element.44), channel_id=1, source_target_pairs={{504,0},{508,4},{0,8},{4,12},{8,16},{12,20},{16,24},{20,28},{24,32... | collective-permute-start | bytes 56 | tf_op jit(solution)/shard_map/ppermute | solution.py:14
  9.7 6.4 %collective-permute-start.2 = (s32[4]{0:T(128)S(1)}, s32[4]{0:T(128)S(1)}, u32[]{:S(2)}, u32[]{:S(2)}) collective-permute-start(s32[4]{0:T(128)S(1)} %get-tuple-element.43), channel_id=1, source_target_pairs={{500,0},{504,4},{508,8},{0,12},{4,16},{8,20},{12,24},{16,28},{20,3... | collective-permute-start | bytes 56 | tf_op jit(solution)/shard_map/ppermute | solution.py:14
  16.1 5.2 %collective-permute-start.3 = (s32[4]{0:T(128)S(1)}, s32[4]{0:T(128)S(1)}, u32[]{:S(2)}, u32[]{:S(2)}) collective-permute-start(s32[4]{0:T(128)S(1)} %get-tuple-element.42), channel_id=1, source_target_pairs={{496,0},{500,4},{504,8},{508,12},{0,16},{4,20},{8,24},{12,28},{16,... | collective-permute-start | bytes 56 | tf_op jit(solution)/shard_map/ppermute | solution.py:14
  25.4 11.3 %all-gather = bf16[32,80]{1,0:T(8,128)(2,1)S(1)} all-gather(bf16[8,80]{1,0:T(8,128)(2,1)S(1)} %fusion.30), channel_id=2, replica_groups=mesh['dom'=128,'blk'=4] {'blk'}, dimensions={0}, use_global_device_ids=true | all-gather | bytes 6400 | tf_op jit(solution)/shard_map/all_gather | solution.py:18
  40.3 10.4 %all-gather.1 = bf16[32,80]{1,0:T(8,128)(2,1)S(1)} all-gather(bf16[8,80]{1,0:T(8,128)(2,1)S(1)} %fusion.40), channel_id=3, replica_groups=mesh['dom'=128,'blk'=4] {'blk'}, dimensions={0}, use_global_device_ids=true | all-gather | bytes 6400 | tf_op jit(solution)/shard_map/all_gather | solution.py:18
  58.1 5.2 %collective-permute-start.7 = (s32[4]{0:T(128)S(1)}, s32[4]{0:T(128)S(1)}, u32[]{:S(2)}, u32[]{:S(2)}) collective-permute-start(s32[4]{0:T(128)S(1)} %get-tuple-element.38), channel_id=1, source_target_pairs={{16,0},{20,4},{24,8},{28,12},{32,16},{36,20},{40,24},{44,28},{48,3... | collective-permute-start | bytes 56 | tf_op jit(solution)/shard_map/ppermute | solution.py:14
  63.4 3.5 %collective-permute-start.8 = (f32[4,320]{1,0:T(4,128)S(1)}, f32[4,320]{1,0:T(4,128)S(1)}, u32[]{:S(2)}, u32[]{:S(2)}) collective-permute-start(f32[4,320]{1,0:T(4,128)S(1)} %get-tuple-element.21), channel_id=1, source_target_pairs={{508,0},{0,4},{4,8},{8,12},{12,16},{16,20},{20,24},{24,28},{28,32}... | collective-permute-start | bytes 15368 | tf_op jit(solution)/shard_map/ppermute | solution.py:14
  69.1 3.9 %collective-permute-start.10 = (f32[4,320]{1,0:T(4,128)S(1)}, f32[4,320]{1,0:T(4,128)S(1)}, u32[]{:S(2)}, u32[]{:S(2)}) collective-permute-start(f32[4,320]{1,0:T(4,128)S(1)} %get-tuple-element.19), channel_id=1, source_target_pairs={{500,0},{504,4},{508,8},{0,12},{4,16},{8,20},{12,24},{16,28},{20,3... | collective-permute-start | bytes 15368 | tf_op jit(solution)/shard_map/ppermute | solution.py:14
  73.0 4.8 %collective-permute-start.11 = (f32[4,320]{1,0:T(4,128)S(1)}, f32[4,320]{1,0:T(4,128)S(1)}, u32[]{:S(2)}, u32[]{:S(2)}) collective-permute-start(f32[4,320]{1,0:T(4,128)S(1)} %get-tuple-element.18), channel_id=1, source_target_pairs={{496,0},{500,4},{504,8},{508,12},{0,16},{4,20},{8,24},{12,28},{16,... | collective-permute-start | bytes 15368 | tf_op jit(solution)/shard_map/ppermute | solution.py:14
  87.9 8.1 %collective-permute-start.18 = (bf16[4,320]{1,0:T(4,128)(2,1)S(1)}, bf16[4,320]{1,0:T(4,128)(2,1)S(1)}, u32[]{:S(2)}, u32[]{:S(2)}) collective-permute-start(bf16[4,320]{1,0:T(4,128)(2,1)S(1)} %get-tuple-element.35), channel_id=1, source_target_pairs={{12,0},{16,4},{20,8},{24,12},{28,16},{32,20},{36,24},{40,28},{44,3... | collective-permute-start | bytes 7688 | tf_op jit(solution)/shard_map/ppermute | solution.py:14
  97.3 3.6 %collective-permute-start.19 = (bf16[4,320]{1,0:T(4,128)(2,1)S(1)}, bf16[4,320]{1,0:T(4,128)(2,1)S(1)}, u32[]{:S(2)}, u32[]{:S(2)}) collective-permute-start(bf16[4,320]{1,0:T(4,128)(2,1)S(1)} %get-tuple-element.34), channel_id=1, source_target_pairs={{16,0},{20,4},{24,8},{28,12},{32,16},{36,20},{40,24},{44,28},{48,3... | collective-permute-start | bytes 7688 | tf_op jit(solution)/shard_map/ppermute | solution.py:14
  100.9 4.0 %collective-permute-done.19 = bf16[4,320]{1,0:T(4,128)(2,1)S(1)} collective-permute-done((bf16[4,320]{1,0:T(4,128)(2,1)S(1)}, bf16[4,320]{1,0:T(4,128)(2,1)S(1)}, u32[]{:S(2)}, u32[]{:S(2)}) %collective-permute-start.19) | collective-permute-done | bytes 2592 | tf_op jit(solution)/shard_map/ppermute | solution.py:14
  106.8 7.2 %collective-permute-done.20 = bf16[4,320]{1,0:T(4,128)(2,1)S(1)} collective-permute-done((bf16[4,320]{1,0:T(4,128)(2,1)S(1)}, bf16[4,320]{1,0:T(4,128)(2,1)S(1)}, u32[]{:S(2)}, u32[]{:S(2)}) %collective-permute-start.20) | collective-permute-done | bytes 2592 | tf_op jit(solution)/shard_map/ppermute | solution.py:14
  116.0 3.5 %collective-permute-done.21 = bf16[4,320]{1,0:T(4,128)(2,1)S(1)} collective-permute-done((bf16[4,320]{1,0:T(4,128)(2,1)S(1)}, bf16[4,320]{1,0:T(4,128)(2,1)S(1)}, u32[]{:S(2)}, u32[]{:S(2)}) %collective-permute-start.21) | collective-permute-done | bytes 2592 | tf_op jit(solution)/shard_map/ppermute | solution.py:14
  121.4 4.4 %collective-permute-done.22 = bf16[4,320]{1,0:T(4,128)(2,1)S(1)} collective-permute-done((bf16[4,320]{1,0:T(4,128)(2,1)S(1)}, bf16[4,320]{1,0:T(4,128)(2,1)S(1)}, u32[]{:S(2)}, u32[]{:S(2)}) %collective-permute-start.22) | collective-permute-done | bytes 2592 | tf_op jit(solution)/shard_map/ppermute | solution.py:14
  128.0 13.6 %collective-permute-done.23 = bf16[4,320]{1,0:T(4,128)(2,1)S(1)} collective-permute-done((bf16[4,320]{1,0:T(4,128)(2,1)S(1)}, bf16[4,320]{1,0:T(4,128)(2,1)S(1)}, u32[]{:S(2)}, u32[]{:S(2)}) %collective-permute-start.23) | collective-permute-done | bytes 2592 | tf_op jit(solution)/shard_map/ppermute | solution.py:14
  145.1 3.4 %collective-permute-start.13 = (f32[4,320]{1,0:T(4,128)S(1)}, f32[4,320]{1,0:T(4,128)S(1)}, u32[]{:S(2)}, u32[]{:S(2)}) collective-permute-start(f32[4,320]{1,0:T(4,128)S(1)} %get-tuple-element.16), channel_id=1, source_target_pairs={{8,0},{12,4},{16,8},{20,12},{24,16},{28,20},{32,24},{36,28},{40,32... | collective-permute-start | bytes 15368 | tf_op jit(solution)/shard_map/ppermute | solution.py:14
  148.5 6.8 %collective-permute-start.14 = (f32[4,320]{1,0:T(4,128)S(1)}, f32[4,320]{1,0:T(4,128)S(1)}, u32[]{:S(2)}, u32[]{:S(2)}) collective-permute-start(f32[4,320]{1,0:T(4,128)S(1)} %get-tuple-element.15), channel_id=1, source_target_pairs={{12,0},{16,4},{20,8},{24,12},{28,16},{32,20},{36,24},{40,28},{44,3... | collective-permute-start | bytes 15368 | tf_op jit(solution)/shard_map/ppermute | solution.py:14
  157.3 5.6 %collective-permute-done.15 = f32[4,320]{1,0:T(4,128)S(1)} collective-permute-done((f32[4,320]{1,0:T(4,128)S(1)}, f32[4,320]{1,0:T(4,128)S(1)}, u32[]{:S(2)}, u32[]{:S(2)}) %collective-permute-start.15) | collective-permute-done | bytes 5152 | tf_op jit(solution)/shard_map/ppermute | solution.py:14
  164.8 15.8 %psum.21 = bf16[8,320]{1,0:T(8,128)(2,1)S(1)} all-reduce(f32[8,320]{1,0:T(8,128)S(1)} %dynamic_update_slice.6), channel_id=1, replica_groups=mesh['dom'=128,'blk'=4] {'blk'}, use_global_device_ids=true, to_apply=%region_7.8 | all-reduce | flops 2560 | bytes 15360 | tf_op jit(solution)/shard_map/psum | solution.py:99
  181.7 10.4 %all-gather.2 = bf16[32,80]{1,0:T(8,128)(2,1)S(1)} all-gather(bf16[8,80]{1,0:T(8,128)(2,1)S(1)} %fusion.31), channel_id=4, replica_groups=mesh['dom'=128,'blk'=4] {'blk'}, dimensions={0}, use_global_device_ids=true | all-gather | bytes 6400 | tf_op jit(solution)/shard_map/all_gather | solution.py:18
  199.9 3.6 %collective-permute-start.25 = (f32[4,320]{1,0:T(4,128)S(1)}, f32[4,320]{1,0:T(4,128)S(1)}, u32[]{:S(2)}, u32[]{:S(2)}) collective-permute-start(f32[4,320]{1,0:T(4,128)S(1)} %get-tuple-element.12), channel_id=1, source_target_pairs={{504,0},{508,4},{0,8},{4,12},{8,16},{12,20},{16,24},{20,28},{24,32... | collective-permute-start | bytes 15368 | tf_op jit(solution)/shard_map/ppermute | solution.py:14
  212.9 5.9 %collective-permute-start.34 = (bf16[4,320]{1,0:T(4,128)(2,1)S(1)}, bf16[4,320]{1,0:T(4,128)(2,1)S(1)}, u32[]{:S(2)}, u32[]{:S(2)}) collective-permute-start(bf16[4,320]{1,0:T(4,128)(2,1)S(1)} %get-tuple-element.27), channel_id=1, source_target_pairs={{12,0},{16,4},{20,8},{24,12},{28,16},{32,20},{36,24},{40,28},{44,3... | collective-permute-start | bytes 7688 | tf_op jit(solution)/shard_map/ppermute | solution.py:14
  220.1 5.3 %collective-permute-start.35 = (bf16[4,320]{1,0:T(4,128)(2,1)S(1)}, bf16[4,320]{1,0:T(4,128)(2,1)S(1)}, u32[]{:S(2)}, u32[]{:S(2)}) collective-permute-start(bf16[4,320]{1,0:T(4,128)(2,1)S(1)} %get-tuple-element.26), channel_id=1, source_target_pairs={{16,0},{20,4},{24,8},{28,12},{32,16},{36,20},{40,24},{44,28},{48,3... | collective-permute-start | bytes 7688 | tf_op jit(solution)/shard_map/ppermute | solution.py:14
  230.8 6.0 %collective-permute-done.36 = bf16[4,320]{1,0:T(4,128)(2,1)S(1)} collective-permute-done((bf16[4,320]{1,0:T(4,128)(2,1)S(1)}, bf16[4,320]{1,0:T(4,128)(2,1)S(1)}, u32[]{:S(2)}, u32[]{:S(2)}) %collective-permute-start.36) | collective-permute-done | bytes 2592 | tf_op jit(solution)/shard_map/ppermute | solution.py:14
  238.8 4.8 %collective-permute-done.37 = bf16[4,320]{1,0:T(4,128)(2,1)S(1)} collective-permute-done((bf16[4,320]{1,0:T(4,128)(2,1)S(1)}, bf16[4,320]{1,0:T(4,128)(2,1)S(1)}, u32[]{:S(2)}, u32[]{:S(2)}) %collective-permute-start.37) | collective-permute-done | bytes 2592 | tf_op jit(solution)/shard_map/ppermute | solution.py:14
  245.5 4.6 %collective-permute-done.38 = bf16[4,320]{1,0:T(4,128)(2,1)S(1)} collective-permute-done((bf16[4,320]{1,0:T(4,128)(2,1)S(1)}, bf16[4,320]{1,0:T(4,128)(2,1)S(1)}, u32[]{:S(2)}, u32[]{:S(2)}) %collective-permute-start.38) | collective-permute-done | bytes 2592 | tf_op jit(solution)/shard_map/ppermute | solution.py:14
  252.1 12.3 %collective-permute-done.39 = bf16[4,320]{1,0:T(4,128)(2,1)S(1)} collective-permute-done((bf16[4,320]{1,0:T(4,128)(2,1)S(1)}, bf16[4,320]{1,0:T(4,128)(2,1)S(1)}, u32[]{:S(2)}, u32[]{:S(2)}) %collective-permute-start.39) | collective-permute-done | bytes 2592 | tf_op jit(solution)/shard_map/ppermute | solution.py:14
  271.3 6.8 %collective-permute-start.30 = (f32[4,320]{1,0:T(4,128)S(1)}, f32[4,320]{1,0:T(4,128)S(1)}, u32[]{:S(2)}, u32[]{:S(2)}) collective-permute-start(f32[4,320]{1,0:T(4,128)S(1)} %get-tuple-element.7), channel_id=1, source_target_pairs={{12,0},{16,4},{20,8},{24,12},{28,16},{32,20},{36,24},{40,28},{44,3... | collective-permute-start | bytes 15368 | tf_op jit(solution)/shard_map/ppermute | solution.py:14
  280.2 5.6 %collective-permute-done.31 = f32[4,320]{1,0:T(4,128)S(1)} collective-permute-done((f32[4,320]{1,0:T(4,128)S(1)}, f32[4,320]{1,0:T(4,128)S(1)}, u32[]{:S(2)}, u32[]{:S(2)}) %collective-permute-start.31) | collective-permute-done | bytes 5152 | tf_op jit(solution)/shard_map/ppermute | solution.py:14
  287.7 14.3 %psum.22 = bf16[8,320]{1,0:T(8,128)(2,1)S(1)} all-reduce(f32[8,320]{1,0:T(8,128)S(1)} %dynamic_update_slice.7), channel_id=1, replica_groups=mesh['dom'=128,'blk'=4] {'blk'}, use_global_device_ids=true, to_apply=%region_12.13 | all-reduce | flops 2560 | bytes 15360 | tf_op jit(solution)/shard_map/psum | solution.py:99
  303.2 9.5 %psum.23 = f32[8]{0:T(128)} all-reduce(f32[8]{0:T(128)S(1)} %get-tuple-element.2), channel_id=1, replica_groups=mesh['dom'=128,'blk'=4] {'blk'}, use_global_device_ids=true, to_apply=%region_14.15 | all-reduce | flops 8 | bytes 64 | tf_op jit(solution)/shard_map/psum | solution.py:103
  (176 shorter events, 91.3 us)
Async XLA Ops:
  4.0 50.2 %collective-permute-start = (s32[4]{0:T(128)S(1)}, s32[4]{0:T(128)S(1)}, u32[]{:S(2)}, u32[]{:S(2)}) collective-permute-start(s32[4]{0:T(128)S(1)} %get-tuple-element.45), channel_id=1, source_target_pairs={{508,0},{0,4},{4,8},{8,12},{12,16},{16,20},{20,24},{24,28},{28,32}... | collective-permute-start | bytes 56 | tf_op jit(solution)/shard_map/ppermute | solution.py:14
  5.9 50.3 %collective-permute-start.1 = (s32[4]{0:T(128)S(1)}, s32[4]{0:T(128)S(1)}, u32[]{:S(2)}, u32[]{:S(2)}) collective-permute-start(s32[4]{0:T(128)S(1)} %get-tuple-element.44), channel_id=1, source_target_pairs={{504,0},{508,4},{0,8},{4,12},{8,16},{12,20},{16,24},{20,28},{24,32... | collective-permute-start | bytes 56 | tf_op jit(solution)/shard_map/ppermute | solution.py:14
  9.7 48.4 %collective-permute-start.2 = (s32[4]{0:T(128)S(1)}, s32[4]{0:T(128)S(1)}, u32[]{:S(2)}, u32[]{:S(2)}) collective-permute-start(s32[4]{0:T(128)S(1)} %get-tuple-element.43), channel_id=1, source_target_pairs={{500,0},{504,4},{508,8},{0,12},{4,16},{8,20},{12,24},{16,28},{20,3... | collective-permute-start | bytes 56 | tf_op jit(solution)/shard_map/ppermute | solution.py:14
  16.1 47.3 %collective-permute-start.3 = (s32[4]{0:T(128)S(1)}, s32[4]{0:T(128)S(1)}, u32[]{:S(2)}, u32[]{:S(2)}) collective-permute-start(s32[4]{0:T(128)S(1)} %get-tuple-element.42), channel_id=1, source_target_pairs={{496,0},{500,4},{504,8},{508,12},{0,16},{4,20},{8,24},{12,28},{16,... | collective-permute-start | bytes 56 | tf_op jit(solution)/shard_map/ppermute | solution.py:14
  21.3 45.5 %collective-permute-start.4 = (s32[4]{0:T(128)S(1)}, s32[4]{0:T(128)S(1)}, u32[]{:S(2)}, u32[]{:S(2)}) collective-permute-start(s32[4]{0:T(128)S(1)} %get-tuple-element.41), channel_id=1, source_target_pairs={{4,0},{8,4},{12,8},{16,12},{20,16},{24,20},{28,24},{32,28},{36,32}... | collective-permute-start | bytes 56 | tf_op jit(solution)/shard_map/ppermute | solution.py:14
  54.2 14.9 %collective-permute-start.5 = (s32[4]{0:T(128)S(1)}, s32[4]{0:T(128)S(1)}, u32[]{:S(2)}, u32[]{:S(2)}) collective-permute-start(s32[4]{0:T(128)S(1)} %get-tuple-element.40), channel_id=1, source_target_pairs={{8,0},{12,4},{16,8},{20,12},{24,16},{28,20},{32,24},{36,28},{40,32... | collective-permute-start | bytes 56 | tf_op jit(solution)/shard_map/ppermute | solution.py:14
  56.2 16.8 %collective-permute-start.6 = (s32[4]{0:T(128)S(1)}, s32[4]{0:T(128)S(1)}, u32[]{:S(2)}, u32[]{:S(2)}) collective-permute-start(s32[4]{0:T(128)S(1)} %get-tuple-element.39), channel_id=1, source_target_pairs={{12,0},{16,4},{20,8},{24,12},{28,16},{32,20},{36,24},{40,28},{44,3... | collective-permute-start | bytes 56 | tf_op jit(solution)/shard_map/ppermute | solution.py:14
  58.1 19.7 %collective-permute-start.7 = (s32[4]{0:T(128)S(1)}, s32[4]{0:T(128)S(1)}, u32[]{:S(2)}, u32[]{:S(2)}) collective-permute-start(s32[4]{0:T(128)S(1)} %get-tuple-element.38), channel_id=1, source_target_pairs={{16,0},{20,4},{24,8},{28,12},{32,16},{36,20},{40,24},{44,28},{48,3... | collective-permute-start | bytes 56 | tf_op jit(solution)/shard_map/ppermute | solution.py:14
  63.4 81.7 %collective-permute-start.8 = (f32[4,320]{1,0:T(4,128)S(1)}, f32[4,320]{1,0:T(4,128)S(1)}, u32[]{:S(2)}, u32[]{:S(2)}) collective-permute-start(f32[4,320]{1,0:T(4,128)S(1)} %get-tuple-element.21), channel_id=1, source_target_pairs={{508,0},{0,4},{4,8},{8,12},{12,16},{16,20},{20,24},{24,28},{28,32}... | collective-permute-start | bytes 15368 | tf_op jit(solution)/shard_map/ppermute | solution.py:14
  66.9 81.6 %collective-permute-start.9 = (f32[4,320]{1,0:T(4,128)S(1)}, f32[4,320]{1,0:T(4,128)S(1)}, u32[]{:S(2)}, u32[]{:S(2)}) collective-permute-start(f32[4,320]{1,0:T(4,128)S(1)} %get-tuple-element.20), channel_id=1, source_target_pairs={{504,0},{508,4},{0,8},{4,12},{8,16},{12,20},{16,24},{20,28},{24,32... | collective-permute-start | bytes 15368 | tf_op jit(solution)/shard_map/ppermute | solution.py:14
  69.1 86.2 %collective-permute-start.10 = (f32[4,320]{1,0:T(4,128)S(1)}, f32[4,320]{1,0:T(4,128)S(1)}, u32[]{:S(2)}, u32[]{:S(2)}) collective-permute-start(f32[4,320]{1,0:T(4,128)S(1)} %get-tuple-element.19), channel_id=1, source_target_pairs={{500,0},{504,4},{508,8},{0,12},{4,16},{8,20},{12,24},{16,28},{20,3... | collective-permute-start | bytes 15368 | tf_op jit(solution)/shard_map/ppermute | solution.py:14
  73.0 84.2 %collective-permute-start.11 = (f32[4,320]{1,0:T(4,128)S(1)}, f32[4,320]{1,0:T(4,128)S(1)}, u32[]{:S(2)}, u32[]{:S(2)}) collective-permute-start(f32[4,320]{1,0:T(4,128)S(1)} %get-tuple-element.18), channel_id=1, source_target_pairs={{496,0},{500,4},{504,8},{508,12},{0,16},{4,20},{8,24},{12,28},{16,... | collective-permute-start | bytes 15368 | tf_op jit(solution)/shard_map/ppermute | solution.py:14
  87.9 9.4 %collective-permute-start.18 = (bf16[4,320]{1,0:T(4,128)(2,1)S(1)}, bf16[4,320]{1,0:T(4,128)(2,1)S(1)}, u32[]{:S(2)}, u32[]{:S(2)}) collective-permute-start(bf16[4,320]{1,0:T(4,128)(2,1)S(1)} %get-tuple-element.35), channel_id=1, source_target_pairs={{12,0},{16,4},{20,8},{24,12},{28,16},{32,20},{36,24},{40,28},{44,3... | collective-permute-start | bytes 7688 | tf_op jit(solution)/shard_map/ppermute | solution.py:14
  97.3 7.6 %collective-permute-start.19 = (bf16[4,320]{1,0:T(4,128)(2,1)S(1)}, bf16[4,320]{1,0:T(4,128)(2,1)S(1)}, u32[]{:S(2)}, u32[]{:S(2)}) collective-permute-start(bf16[4,320]{1,0:T(4,128)(2,1)S(1)} %get-tuple-element.34), channel_id=1, source_target_pairs={{16,0},{20,4},{24,8},{28,12},{32,16},{36,20},{40,24},{44,28},{48,3... | collective-permute-start | bytes 7688 | tf_op jit(solution)/shard_map/ppermute | solution.py:14
  104.9 9.2 %collective-permute-start.20 = (bf16[4,320]{1,0:T(4,128)(2,1)S(1)}, bf16[4,320]{1,0:T(4,128)(2,1)S(1)}, u32[]{:S(2)}, u32[]{:S(2)}) collective-permute-start(bf16[4,320]{1,0:T(4,128)(2,1)S(1)} %get-tuple-element.33), channel_id=1, source_target_pairs={{508,0},{0,4},{4,8},{8,12},{12,16},{16,20},{20,24},{24,28},{28,32}... | collective-permute-start | bytes 7688 | tf_op jit(solution)/shard_map/ppermute | solution.py:14
  125.9 15.7 %collective-permute-start.23 = (bf16[4,320]{1,0:T(4,128)(2,1)S(1)}, bf16[4,320]{1,0:T(4,128)(2,1)S(1)}, u32[]{:S(2)}, u32[]{:S(2)}) collective-permute-start(bf16[4,320]{1,0:T(4,128)(2,1)S(1)} %get-tuple-element.30), channel_id=1, source_target_pairs={{496,0},{500,4},{504,8},{508,12},{0,16},{4,20},{8,24},{12,28},{16,... | collective-permute-start | bytes 7688 | tf_op jit(solution)/shard_map/ppermute | solution.py:14
  141.6 15.6 %collective-permute-start.12 = (f32[4,320]{1,0:T(4,128)S(1)}, f32[4,320]{1,0:T(4,128)S(1)}, u32[]{:S(2)}, u32[]{:S(2)}) collective-permute-start(f32[4,320]{1,0:T(4,128)S(1)} %get-tuple-element.17), channel_id=1, source_target_pairs={{4,0},{8,4},{12,8},{16,12},{20,16},{24,20},{28,24},{32,28},{36,32}... | collective-permute-start | bytes 15368 | tf_op jit(solution)/shard_map/ppermute | solution.py:14
  145.1 12.2 %collective-permute-start.13 = (f32[4,320]{1,0:T(4,128)S(1)}, f32[4,320]{1,0:T(4,128)S(1)}, u32[]{:S(2)}, u32[]{:S(2)}) collective-permute-start(f32[4,320]{1,0:T(4,128)S(1)} %get-tuple-element.16), channel_id=1, source_target_pairs={{8,0},{12,4},{16,8},{20,12},{24,16},{28,20},{32,24},{36,28},{40,32... | collective-permute-start | bytes 15368 | tf_op jit(solution)/shard_map/ppermute | solution.py:14
  148.5 8.8 %collective-permute-start.14 = (f32[4,320]{1,0:T(4,128)S(1)}, f32[4,320]{1,0:T(4,128)S(1)}, u32[]{:S(2)}, u32[]{:S(2)}) collective-permute-start(f32[4,320]{1,0:T(4,128)S(1)} %get-tuple-element.15), channel_id=1, source_target_pairs={{12,0},{16,4},{20,8},{24,12},{28,16},{32,20},{36,24},{40,28},{44,3... | collective-permute-start | bytes 15368 | tf_op jit(solution)/shard_map/ppermute | solution.py:14
  155.3 7.6 %collective-permute-start.15 = (f32[4,320]{1,0:T(4,128)S(1)}, f32[4,320]{1,0:T(4,128)S(1)}, u32[]{:S(2)}, u32[]{:S(2)}) collective-permute-start(f32[4,320]{1,0:T(4,128)S(1)} %get-tuple-element.14), channel_id=1, source_target_pairs={{16,0},{20,4},{24,8},{28,12},{32,16},{36,20},{40,24},{44,28},{48,3... | collective-permute-start | bytes 15368 | tf_op jit(solution)/shard_map/ppermute | solution.py:14
  194.1 13.3 %collective-permute-start.32 = (bf16[4,320]{1,0:T(4,128)(2,1)S(1)}, bf16[4,320]{1,0:T(4,128)(2,1)S(1)}, u32[]{:S(2)}, u32[]{:S(2)}) collective-permute-start(bf16[4,320]{1,0:T(4,128)(2,1)S(1)} %get-tuple-element.29), channel_id=1, source_target_pairs={{4,0},{8,4},{12,8},{16,12},{20,16},{24,20},{28,24},{32,28},{36,32}... | collective-permute-start | bytes 7688 | tf_op jit(solution)/shard_map/ppermute | solution.py:14
  197.5 70.4 %collective-permute-start.24 = (f32[4,320]{1,0:T(4,128)S(1)}, f32[4,320]{1,0:T(4,128)S(1)}, u32[]{:S(2)}, u32[]{:S(2)}) collective-permute-start(f32[4,320]{1,0:T(4,128)S(1)} %get-tuple-element.13), channel_id=1, source_target_pairs={{508,0},{0,4},{4,8},{8,12},{12,16},{16,20},{20,24},{24,28},{28,32}... | collective-permute-start | bytes 15368 | tf_op jit(solution)/shard_map/ppermute | solution.py:14
  199.9 71.4 %collective-permute-start.25 = (f32[4,320]{1,0:T(4,128)S(1)}, f32[4,320]{1,0:T(4,128)S(1)}, u32[]{:S(2)}, u32[]{:S(2)}) collective-permute-start(f32[4,320]{1,0:T(4,128)S(1)} %get-tuple-element.12), channel_id=1, source_target_pairs={{504,0},{508,4},{0,8},{4,12},{8,16},{12,20},{16,24},{20,28},{24,32... | collective-permute-start | bytes 15368 | tf_op jit(solution)/shard_map/ppermute | solution.py:14
  203.6 74.6 %collective-permute-start.26 = (f32[4,320]{1,0:T(4,128)S(1)}, f32[4,320]{1,0:T(4,128)S(1)}, u32[]{:S(2)}, u32[]{:S(2)}) collective-permute-start(f32[4,320]{1,0:T(4,128)S(1)} %get-tuple-element.11), channel_id=1, source_target_pairs={{500,0},{504,4},{508,8},{0,12},{4,16},{8,20},{12,24},{16,28},{20,3... | collective-permute-start | bytes 15368 | tf_op jit(solution)/shard_map/ppermute | solution.py:14
  205.5 74.6 %collective-permute-start.27 = (f32[4,320]{1,0:T(4,128)S(1)}, f32[4,320]{1,0:T(4,128)S(1)}, u32[]{:S(2)}, u32[]{:S(2)}) collective-permute-start(f32[4,320]{1,0:T(4,128)S(1)} %get-tuple-element.10), channel_id=1, source_target_pairs={{496,0},{500,4},{504,8},{508,12},{0,16},{4,20},{8,24},{12,28},{16,... | collective-permute-start | bytes 15368 | tf_op jit(solution)/shard_map/ppermute | solution.py:14
  220.1 7.6 %collective-permute-start.35 = (bf16[4,320]{1,0:T(4,128)(2,1)S(1)}, bf16[4,320]{1,0:T(4,128)(2,1)S(1)}, u32[]{:S(2)}, u32[]{:S(2)}) collective-permute-start(bf16[4,320]{1,0:T(4,128)(2,1)S(1)} %get-tuple-element.26), channel_id=1, source_target_pairs={{16,0},{20,4},{24,8},{28,12},{32,16},{36,20},{40,24},{44,28},{48,3... | collective-permute-start | bytes 7688 | tf_op jit(solution)/shard_map/ppermute | solution.py:14
  227.7 9.2 %collective-permute-start.36 = (bf16[4,320]{1,0:T(4,128)(2,1)S(1)}, bf16[4,320]{1,0:T(4,128)(2,1)S(1)}, u32[]{:S(2)}, u32[]{:S(2)}) collective-permute-start(bf16[4,320]{1,0:T(4,128)(2,1)S(1)} %get-tuple-element.25), channel_id=1, source_target_pairs={{508,0},{0,4},{4,8},{8,12},{12,16},{16,20},{20,24},{24,28},{28,32}... | collective-permute-start | bytes 7688 | tf_op jit(solution)/shard_map/ppermute | solution.py:14
  250.2 14.3 %collective-permute-start.39 = (bf16[4,320]{1,0:T(4,128)(2,1)S(1)}, bf16[4,320]{1,0:T(4,128)(2,1)S(1)}, u32[]{:S(2)}, u32[]{:S(2)}) collective-permute-start(bf16[4,320]{1,0:T(4,128)(2,1)S(1)} %get-tuple-element.22), channel_id=1, source_target_pairs={{496,0},{500,4},{504,8},{508,12},{0,16},{4,20},{8,24},{12,28},{16,... | collective-permute-start | bytes 7688 | tf_op jit(solution)/shard_map/ppermute | solution.py:14
  264.5 15.6 %collective-permute-start.28 = (f32[4,320]{1,0:T(4,128)S(1)}, f32[4,320]{1,0:T(4,128)S(1)}, u32[]{:S(2)}, u32[]{:S(2)}) collective-permute-start(f32[4,320]{1,0:T(4,128)S(1)} %get-tuple-element.9), channel_id=1, source_target_pairs={{4,0},{8,4},{12,8},{16,12},{20,16},{24,20},{28,24},{32,28},{36,32}... | collective-permute-start | bytes 15368 | tf_op jit(solution)/shard_map/ppermute | solution.py:14
  267.9 12.2 %collective-permute-start.29 = (f32[4,320]{1,0:T(4,128)S(1)}, f32[4,320]{1,0:T(4,128)S(1)}, u32[]{:S(2)}, u32[]{:S(2)}) collective-permute-start(f32[4,320]{1,0:T(4,128)S(1)} %get-tuple-element.8), channel_id=1, source_target_pairs={{8,0},{12,4},{16,8},{20,12},{24,16},{28,20},{32,24},{36,28},{40,32... | collective-permute-start | bytes 15368 | tf_op jit(solution)/shard_map/ppermute | solution.py:14
  271.3 8.8 %collective-permute-start.30 = (f32[4,320]{1,0:T(4,128)S(1)}, f32[4,320]{1,0:T(4,128)S(1)}, u32[]{:S(2)}, u32[]{:S(2)}) collective-permute-start(f32[4,320]{1,0:T(4,128)S(1)} %get-tuple-element.7), channel_id=1, source_target_pairs={{12,0},{16,4},{20,8},{24,12},{28,16},{32,20},{36,24},{40,28},{44,3... | collective-permute-start | bytes 15368 | tf_op jit(solution)/shard_map/ppermute | solution.py:14
  278.1 7.6 %collective-permute-start.31 = (f32[4,320]{1,0:T(4,128)S(1)}, f32[4,320]{1,0:T(4,128)S(1)}, u32[]{:S(2)}, u32[]{:S(2)}) collective-permute-start(f32[4,320]{1,0:T(4,128)S(1)} %get-tuple-element.6), channel_id=1, source_target_pairs={{16,0},{20,4},{24,8},{28,12},{32,16},{36,20},{40,24},{44,28},{48,3... | collective-permute-start | bytes 15368 | tf_op jit(solution)/shard_map/ppermute | solution.py:14
  (12 other events, 271.6 us)
